TPU v7x, 512 devices: a whole 4x4x16 slice. The times are simulated.
512 devices in a mesh: req: 64 (over z, y), head: 8 (over x, core).
Axes of the slice: x: 4, y: 4, z: 16, core: 2. Of those that a mesh axis runs over, the one named last changes fastest.
Arguments:
- inner_input: bfloat16 [16384, 16384], P('req', 'head'), may hold values from -6 to 6
- projection_input: bfloat16 [16384, 8, 2, 128], P('req', 'head'), may hold values from -6 to 6
- step_before_bias: bfloat16 [16384, 256], P('req', 'head'), may hold values from -2 to 11
- inner_conv_taps: float32 [4, 16384], P(None, 'head'), may hold values from -3 to 3
- projection_conv_taps: float32 [4, 8, 2, 128], P(None, 'head'), may hold values from -3 to 3
- step_bias: float32 [256], P('head'), may hold values from -4.5 to -3.5
- head_decay_rate: float32 [256], P('head'), may hold values from 0.1 to 3
- head_skip_gain: float32 [256], P('head'), may hold values from 0.5 to 1.5
- group_norm_gain: float32 [16384], P('head'), may hold values from 0.5 to 1.5
- tenant: int32 [64], P('req'), may hold values from 0 to 63
- tenant_adapter_row: int32 [64], replicated, may hold values from 0 to 63, each once
- cache_holder_index: int32 [64], P('req'), may hold values from 0 to 63, as said below
- cache_slot_index: int32 [64], P('req'), may hold values from 0 to 1
- adapter_down_panels: bfloat16 [64, 16384, 64], P('req', 'head'), may hold values from -0.046875 to 0.046875
- adapter_up_panels: bfloat16 [64, 64, 8192], P('req', None, 'head'), may hold values from -0.75 to 0.75
- cached_ssm_states: bfloat16 [128, 256, 64, 128], P('req', 'head'), may hold values from -2.5 to 2.5
- inner_conv_cache: bfloat16 [128, 3, 16384], P('req', None, 'head'), may hold values from -6 to 6
- projection_conv_cache: bfloat16 [128, 3, 8, 2, 128], P('req', None, 'head'), may hold values from -6 to 6
Outputs:
- normed_output: bfloat16 [16384, 16384], P('req', 'head')
- adapter_output_term: bfloat16 [16384, 8192], P('req', 'head')
- updated_state: bfloat16 [64, 256, 64, 128], P('req', 'head')
Inputs may be any that keep to these rules, and one draw needn't show every extreme that they name: `tenant_adapter_row`: every row of the adapter tables belongs to exactly one tenant. `cache_holder_index`: no two requests share a cache slot, and each index of req holds the cached states of exactly 1 request.
All inputs are finite; a program needn't handle non-finite values.
Results may differ from a plain program's by a relative error of at most 0.013.
Values may be sent and summed in bfloat16 or wider, within the bound.
No kernel may reach another device: no remote copies, remote signals or barrier semaphores. Data moves between devices by JAX's collectives and lax.ppermute only.
A program may use at most 64 MiB of HBM per device.

v0:
```python
import jax
import jax.numpy as jnp
from jax import lax
from jax.sharding import PartitionSpec as P

ADAPTER_SCALE = 2.0
NORM_EPSILON = 1e-05


def causal_conv(cached, current, weight):
    joined = jnp.concatenate([cached, current], axis=1)
    length_value = current.shape[1]
    summed = weight[0] * joined[:, 0:length_value]
    for tap in range(1, weight.shape[0]):
        summed = summed + weight[tap] * joined[:, tap : tap + length_value]
    return jax.nn.silu(summed).astype(jnp.bfloat16)


def per_device(
    inner_input,
    projection_input,
    step_before_bias,
    inner_conv_taps,
    projection_conv_taps,
    step_bias,
    head_decay_rate,
    head_skip_gain,
    group_norm_gain,
    tenant,
    tenant_adapter_row,
    cache_holder_index,
    cache_slot_index,
    adapter_down_panels,
    adapter_up_panels,
    cached_ssm_states,
    inner_conv_cache,
    projection_conv_cache,
):
    per_device_share = tenant.shape[0]
    slots_dev = cached_ssm_states.shape[0]
    hidden_features_on_card = inner_input.shape[1]
    heads_dev = step_before_bias.shape[1]
    groups_dev = projection_input.shape[1]
    state_size = projection_input.shape[3]
    head_size = hidden_features_on_card // heads_dev
    per_group = heads_dev // groups_dev
    reduced_width = adapter_down_panels.shape[2]
    model_per_device = adapter_up_panels.shape[2]
    tap_count = inner_conv_taps.shape[0]
    length_value = inner_input.shape[0] // per_device_share
    tenant_all, owner_all, slot_all = (
        lax.all_gather(tenant, "req", axis=0, tiled=True),
        lax.all_gather(cache_holder_index, "req", axis=0, tiled=True),
        lax.all_gather(cache_slot_index, "req", axis=0, tiled=True),
    )
    customer_identifiers = jnp.arange(tenant_adapter_row.shape[0], dtype=jnp.int32)
    picked_customer_matrix_pair = jnp.sum(
        jnp.where(
            tenant_all[:, None] == customer_identifiers[None, :], tenant_adapter_row[None, :], 0
        ),
        axis=1,
    )
    ssm_flat = cached_ssm_states.reshape(slots_dev, -1)
    convx_flat = inner_conv_cache.reshape(slots_dev, -1)
    convbc_flat = projection_conv_cache.reshape(slots_dev, -1)
    cache_pick = owner_all * slots_dev + slot_all
    dispersion_factor = (
        lax.all_to_all(
            adapter_down_panels.reshape(adapter_down_panels.shape[0], -1),
            "req",
            split_axis=1,
            concat_axis=0,
            tiled=True,
        ),
        lax.all_to_all(
            adapter_up_panels.reshape(adapter_up_panels.shape[0], -1),
            "req",
            split_axis=1,
            concat_axis=0,
            tiled=True,
        ),
        lax.all_to_all(ssm_flat, "req", split_axis=1, concat_axis=0, tiled=True),
        lax.all_to_all(convx_flat, "req", split_axis=1, concat_axis=0, tiled=True),
        lax.all_to_all(convbc_flat, "req", split_axis=1, concat_axis=0, tiled=True),
    )
    picked_left_factor = jnp.take(dispersion_factor[0], picked_customer_matrix_pair, axis=0)
    picked_right_factor = jnp.take(dispersion_factor[1], picked_customer_matrix_pair, axis=0)
    chosen_state = jnp.take(dispersion_factor[2], cache_pick, axis=0)
    chosen_convx = jnp.take(dispersion_factor[3], cache_pick, axis=0)
    chosen_convbc = jnp.take(dispersion_factor[4], cache_pick, axis=0)
    fetched = (
        lax.all_to_all(picked_left_factor, "req", split_axis=0, concat_axis=1, tiled=True),
        lax.all_to_all(picked_right_factor, "req", split_axis=0, concat_axis=1, tiled=True),
        lax.all_to_all(chosen_state, "req", split_axis=0, concat_axis=1, tiled=True),
        lax.all_to_all(chosen_convx, "req", split_axis=0, concat_axis=1, tiled=True),
        lax.all_to_all(chosen_convbc, "req", split_axis=0, concat_axis=1, tiled=True),
    )
    down_panel = fetched[0].reshape(per_device_share, hidden_features_on_card, reduced_width)
    up_panel = fetched[1].reshape(per_device_share, reduced_width, model_per_device)
    cached_state = fetched[2].reshape(
        per_device_share, groups_dev, per_group, head_size, state_size
    )
    cached_x = fetched[3].reshape(per_device_share, tap_count - 1, hidden_features_on_card)
    cached_bc = fetched[4].reshape(per_device_share, tap_count - 1, groups_dev, 2, state_size)
    conv_x = causal_conv(
        cached_x,
        inner_input.reshape(per_device_share, length_value, hidden_features_on_card),
        inner_conv_taps,
    )
    conv_bc = causal_conv(
        cached_bc,
        projection_input.reshape(per_device_share, length_value, groups_dev, 2, state_size),
        projection_conv_taps,
    )
    b_proj = conv_bc[:, :, :, 0]
    c_proj = conv_bc[:, :, :, 1]
    step_size = jax.nn.softplus(step_before_bias.astype(jnp.float32) + step_bias).reshape(
        per_device_share, length_value, heads_dev
    )
    log_decay = jnp.cumsum(-head_decay_rate * step_size, axis=1)
    log_decay5 = log_decay.reshape(per_device_share, length_value, groups_dev, per_group)
    step_size5 = step_size.reshape(per_device_share, length_value, groups_dev, per_group)
    score_bc = jnp.einsum("rtgn,rsgn->rgts", c_proj, b_proj, preferred_element_type=jnp.float32)
    decay_rows = jnp.transpose(log_decay5, (0, 2, 3, 1))
    log_gap = decay_rows[..., :, None] - decay_rows[..., None, :]
    token_ids = jnp.arange(length_value, dtype=jnp.int32)
    causal = token_ids[:, None] >= token_ids[None, :]
    decay_factor = jnp.exp(jnp.where(causal, log_gap, -jnp.inf))
    step_rows = jnp.transpose(step_size5, (0, 2, 3, 1))
    mix_weights = (score_bc[:, :, None] * decay_factor * step_rows[..., None, :]).astype(
        jnp.bfloat16
    )
    conv_heads = conv_x.reshape(per_device_share, length_value, groups_dev, per_group, head_size)
    intra = jnp.einsum(
        "rghts,rsghp->rtghp", mix_weights, conv_heads, preferred_element_type=jnp.float32
    )
    inter = (
        jnp.einsum("rtgn,rghpn->rtghp", c_proj, cached_state, preferred_element_type=jnp.float32)
        * jnp.exp(log_decay5)[..., None]
    )
    skip_gain = head_skip_gain.reshape(groups_dev, per_group)[..., None]
    mixed = intra + inter + skip_gain * conv_heads
    mean_square = jnp.mean(mixed * mixed, axis=(3, 4), keepdims=True)
    normed_output = (
        (mixed * lax.rsqrt(mean_square + NORM_EPSILON)).reshape(
            per_device_share, length_value, hidden_features_on_card
        )
        * group_norm_gain
    ).astype(jnp.bfloat16)
    low_partial = jnp.einsum(
        "rtc,rcq->rtq", normed_output, down_panel, preferred_element_type=jnp.float32
    )
    reduced_rank = lax.psum(low_partial, "head").astype(jnp.bfloat16)
    adapter_output_term = (
        jnp.einsum("rtq,rqd->rtd", reduced_rank, up_panel, preferred_element_type=jnp.float32)
        * ADAPTER_SCALE
    ).astype(jnp.bfloat16)
    log_total = log_decay[:, -1:, :]
    carry_weight = (jnp.exp(log_total - log_decay) * step_size).reshape(
        per_device_share, length_value, groups_dev, per_group
    )
    carried = (conv_heads * carry_weight[..., None]).astype(jnp.bfloat16)
    fresh_state = jnp.einsum(
        "rsghp,rsgn->rghpn", carried, b_proj, preferred_element_type=jnp.float32
    )
    keep_factor = jnp.exp(log_total[:, 0]).reshape(per_device_share, groups_dev, per_group)[
        ..., None, None
    ]
    updated_state = fresh_state + keep_factor * cached_state
    return (
        normed_output.reshape(per_device_share * length_value, hidden_features_on_card),
        adapter_output_term.reshape(per_device_share * length_value, model_per_device),
        updated_state.reshape(per_device_share, heads_dev, head_size, state_size).astype(
            jnp.bfloat16
        ),
    )


def solution(mesh):
    return jax.shard_map(
        per_device,
        mesh=mesh,
        in_specs=(
            P("req", "head"),
            P("req", "head", None, None),
            P("req", "head"),
            P(None, "head"),
            P(None, "head", None, None),
            P("head"),
            P("head"),
            P("head"),
            P("head"),
            P("req"),
            P(),
            P("req"),
            P("req"),
            P("req", "head", None),
            P("req", None, "head"),
            P("req", "head", None, None),
            P("req", None, "head"),
            P("req", None, "head", None, None),
        ),
        out_specs=(P("req", "head"), P("req", "head"), P("req", "head", None, None)),
        check_vma=False,
    )
```

profile of v0, /device:TPU:16, one launch (start us, length us, event | category | flops | bytes accessed | tf_op | source)
XLA Modules:
  0.0 330.3 jit_solution(10483867477987839845)
XLA Ops:
  2.1 18.6 %all-to-all-start.2 = ((bf16[2,64,12]{2,0,1:T(2,128)(2,1)}), bf16[2,64,12]{2,0,1:T(2,128)(2,1)S(1)}, u32[]{:S(2)}, u32[]{:S(2)}) async-start(bf16[2,64,12]{2,0,1:T(2,128)(2,1)} %copy.93), calls=%async_computation.2 | async-start | bytes 65536 | tf_op jit(solution)/shard_map/all_to_all | solution.py:84
  26.2 25.0 %all-reduce.3 = (s32[64]{0:T(128)S(1)}, s32[64]{0:T(128)S(1)}, s32[64]{0:T(128)S(1)}) all-reduce(s32[64]{0:T(128)S(1)} %dynamic-update-slice.1, s32[64]{0:T(128)S(1)} %dynamic-update-slice, s32[64]{0:T(128)S(1)} %dynamic-update-slice.2), channel_id=1, replica_groups=mesh['req'=64,'head'=8] {'req'}, use_global_device_ids=true, to_apply=%add.1 | all-reduce | flops 192 | bytes 1536
  57.5 13.3 %all-to-all-start = ((bf16[2,64,96]{2,0,1:T(2,128)(2,1)}), bf16[2,64,96]{2,0,1:T(2,128)(2,1)S(1)}, u32[]{:S(2)}, u32[]{:S(2)}) async-start(bf16[2,64,96]{2,0,1:T(2,128)(2,1)} %copy.88), calls=%async_computation | async-start | bytes 65536 | tf_op jit(solution)/shard_map/all_to_all | solution.py:83
  70.8 12.8 %all-to-all-done = bf16[2,64,96]{2,0,1:T(2,128)(2,1)S(1)} async-done(((bf16[2,64,96]{2,0,1:T(2,128)(2,1)}), bf16[2,64,96]{2,0,1:T(2,128)(2,1)S(1)}, u32[]{:S(2)}, u32[]{:S(2)}) %all-to-all-start) | async-done | bytes 24608 | tf_op jit(solution)/shard_map/all_to_all | solution.py:83
  83.6 6.2 %all-to-all-start.8 = ((bf16[64,2,512]{2,1,0:T(2,128)(2,1)}), bf16[64,2,512]{2,1,0:T(2,128)(2,1)S(1)}, u32[]{:S(2)}, u32[]{:S(2)}) async-start(bf16[64,2,512]{2,1,0:T(2,128)(2,1)} %reshape.580), calls=%async_computation.8 | async-start | bytes 262144 | tf_op jit(solution)/shard_map/all_to_all | solution.py:75
  91.9 12.9 %all-to-all-done.8 = bf16[64,2,512]{2,1,0:T(2,128)(2,1)S(1)} async-done(((bf16[64,2,512]{2,1,0:T(2,128)(2,1)}), bf16[64,2,512]{2,1,0:T(2,128)(2,1)S(1)}, u32[]{:S(2)}, u32[]{:S(2)}) %all-to-all-start.8) | async-done | bytes 131104 | tf_op jit(solution)/shard_map/all_to_all | solution.py:75
  104.8 5.9 %all-to-all-start.3 = ((bf16[64,1,12]{2,1,0:T(2,128)(2,1)}), bf16[64,1,12]{2,1,0:T(2,128)(2,1)S(1)}, u32[]{:S(2)}, u32[]{:S(2)}) async-start(bf16[64,1,12]{2,1,0:T(2,128)(2,1)} %copy.94), calls=%async_computation.3 | async-start | bytes 65536 | tf_op jit(solution)/shard_map/all_to_all | solution.py:96
  112.3 11.3 %all-to-all-done.3 = bf16[64,1,12]{2,1,0:T(2,128)(2,1)S(1)} async-done(((bf16[64,1,12]{2,1,0:T(2,128)(2,1)}), bf16[64,1,12]{2,1,0:T(2,128)(2,1)S(1)}, u32[]{:S(2)}, u32[]{:S(2)}) %all-to-all-start.3) | async-done | bytes 1568 | tf_op jit(solution)/shard_map/all_to_all | solution.py:96
  123.6 6.3 %all-to-all-start.1 = ((bf16[64,1,96]{2,1,0:T(2,128)(2,1)}), bf16[64,1,96]{2,1,0:T(2,128)(2,1)S(1)}, u32[]{:S(2)}, u32[]{:S(2)}) async-start(bf16[64,1,96]{2,1,0:T(2,128)(2,1)} %copy.89), calls=%async_computation.1 | async-start | bytes 65536 | tf_op jit(solution)/shard_map/all_to_all | solution.py:95
  131.5 11.3 %all-to-all-done.1 = bf16[64,1,96]{2,1,0:T(2,128)(2,1)S(1)} async-done(((bf16[64,1,96]{2,1,0:T(2,128)(2,1)}), bf16[64,1,96]{2,1,0:T(2,128)(2,1)S(1)}, u32[]{:S(2)}, u32[]{:S(2)}) %all-to-all-start.1) | async-done | bytes 12320 | tf_op jit(solution)/shard_map/all_to_all | solution.py:95
  142.9 6.4 %all-to-all-start.9 = ((bf16[64,2,512]{2,1,0:T(2,128)(2,1)}), bf16[64,2,512]{2,1,0:T(2,128)(2,1)S(1)}, u32[]{:S(2)}, u32[]{:S(2)}) async-start(bf16[64,2,512]{2,1,0:T(2,128)(2,1)} %reshape.582), calls=%async_computation.9 | async-start | bytes 262144 | tf_op jit(solution)/shard_map/all_to_all | solution.py:93
  153.0 10.8 %all-to-all-done.9 = bf16[64,2,512]{2,1,0:T(2,128)(2,1)S(1)} async-done(((bf16[64,2,512]{2,1,0:T(2,128)(2,1)}), bf16[64,2,512]{2,1,0:T(2,128)(2,1)S(1)}, u32[]{:S(2)}, u32[]{:S(2)}) %all-to-all-start.9) | async-done | bytes 131104 | tf_op jit(solution)/shard_map/all_to_all | solution.py:93
  164.4 6.6 %all-to-all-start.6 = ((bf16[64,2,1024]{2,1,0:T(2,128)(2,1)}), bf16[64,2,1024]{2,1,0:T(2,128)(2,1)S(1)}, u32[]{:S(2)}, u32[]{:S(2)}) async-start(bf16[64,2,1024]{2,1,0:T(2,128)(2,1)} %reshape.584), calls=%async_computation.6 | async-start | bytes 524288 | tf_op jit(solution)/shard_map/all_to_all | solution.py:68
  173.7 14.8 %all-to-all-done.6 = bf16[64,2,1024]{2,1,0:T(2,128)(2,1)S(1)} async-done(((bf16[64,2,1024]{2,1,0:T(2,128)(2,1)}), bf16[64,2,1024]{2,1,0:T(2,128)(2,1)S(1)}, u32[]{:S(2)}, u32[]{:S(2)}) %all-to-all-start.6) | async-done | bytes 262176 | tf_op jit(solution)/shard_map/all_to_all | solution.py:68
  188.4 6.1 %all-to-all-start.4 = ((bf16[2,64,4096]{2,0,1:T(2,128)(2,1)}), bf16[2,64,4096]{2,0,1:T(2,128)(2,1)S(1)}, u32[]{:S(2)}, u32[]{:S(2)}) async-start(bf16[2,64,4096]{2,0,1:T(2,128)(2,1)} %copy.100), calls=%async_computation.4 | async-start | bytes 2097152 | tf_op jit(solution)/shard_map/all_to_all | solution.py:82
  198.8 38.3 %all-to-all-done.4 = bf16[2,64,4096]{2,0,1:T(2,128)(2,1)S(1)} async-done(((bf16[2,64,4096]{2,0,1:T(2,128)(2,1)}), bf16[2,64,4096]{2,0,1:T(2,128)(2,1)S(1)}, u32[]{:S(2)}, u32[]{:S(2)}) %all-to-all-start.4) | async-done | bytes 1048608 | tf_op jit(solution)/shard_map/all_to_all | solution.py:82
  237.1 5.9 %all-to-all-start.7 = ((bf16[64,2,1024]{2,1,0:T(2,128)(2,1)}), bf16[64,2,1024]{2,1,0:T(2,128)(2,1)S(1)}, u32[]{:S(2)}, u32[]{:S(2)}) async-start(bf16[64,2,1024]{2,1,0:T(2,128)(2,1)} %reshape.586), calls=%async_computation.7 | async-start | bytes 524288 | tf_op jit(solution)/shard_map/all_to_all | solution.py:92
  247.0 13.4 %all-to-all-done.7 = bf16[64,2,1024]{2,1,0:T(2,128)(2,1)S(1)} async-done(((bf16[64,2,1024]{2,1,0:T(2,128)(2,1)}), bf16[64,2,1024]{2,1,0:T(2,128)(2,1)S(1)}, u32[]{:S(2)}, u32[]{:S(2)}) %all-to-all-start.7) | async-done | bytes 262176 | tf_op jit(solution)/shard_map/all_to_all | solution.py:92
  260.4 5.8 %all-to-all-start.5 = ((bf16[64,2,2048]{2,1,0:T(2,128)(2,1)}), bf16[64,2,2048]{2,1,0:T(2,128)(2,1)S(1)}, u32[]{:S(2)}, u32[]{:S(2)}) async-start(bf16[64,2,2048]{2,1,0:T(2,128)(2,1)} %reshape.578), calls=%async_computation.5 | async-start | bytes 1048576 | tf_op jit(solution)/shard_map/all_to_all | solution.py:94
  272.2 3.8 %fusion.9 = (bf16[1,256,2048]{1,2,0:T(8,128)(2,1)}, bf16[1,256,2048]{1,2,0:T(8,128)(2,1)}) fusion(f32[256,32]{0,1:T(8,128)S(1)} %bitcast.165, bf16[256,2048]{0,1:T(8,128)(2,1)S(1)} %copy.90, f32[2048]{0:T(1024)S(1)} %bitcast.169, bf16[1,256,2048]{1,2,0:T(8,128)(2,1)S(1)} %bitcast.147, bf16[1,3,2048]{1,2,0:T(8,128)(2,1)S(1)} %copy.91, f32[2048]{0:T(1024)S(1)} %bitcast.170, ...), kind=kLoop, calls=%fused_computation.17 | loop fusion | flops 14680064 | bytes 4272128 | tf_op jit(solution)/shard_map/convert_element_type | solution.py:162
  278.4 11.4 %all-to-all-done.5 = bf16[64,2,2048]{2,1,0:T(2,128)(2,1)S(1)} async-done(((bf16[64,2,2048]{2,1,0:T(2,128)(2,1)}), bf16[64,2,2048]{2,1,0:T(2,128)(2,1)S(1)}, u32[]{:S(2)}, u32[]{:S(2)}) %all-to-all-start.5) | async-done | bytes 524320 | tf_op jit(solution)/shard_map/all_to_all | solution.py:94
  290.3 3.1 reduce.4
  298.8 24.5 %psum.7 = bf16[1,256,64]{1,2,0:T(8,128)(2,1)S(1)} all-reduce(f32[1,256,64]{1,2,0:T(8,128)} %convolution_bitcast_fusion), channel_id=1, replica_groups=mesh['req'=64,'head'=8] {'head'}, use_global_device_ids=true, to_apply=%region_4.5 | all-reduce | flops 16384 | bytes 98304 | tf_op jit(solution)/shard_map/psum | solution.py:153
  325.2 2.8 multiply_convert_fusion.3
  (142 shorter events, 49.4 us)
Async XLA Ops:
  2.1 55.4 %all-to-all-start.2 = ((bf16[2,64,12]{2,0,1:T(2,128)(2,1)}), bf16[2,64,12]{2,0,1:T(2,128)(2,1)S(1)}, u32[]{:S(2)}, u32[]{:S(2)}) async-start(bf16[2,64,12]{2,0,1:T(2,128)(2,1)} %copy.93), calls=%async_computation.2 | async-start | bytes 65536 | tf_op jit(solution)/shard_map/all_to_all | solution.py:84
  56.7 92.5 %copy-start.6 = (bf16[1,2048,64]{1,2,0:T(8,128)(2,1)S(1)}, bf16[1,2048,64]{1,2,0:T(8,128)(2,1)}, u32[]{:S(2)}) copy-start(bf16[1,2048,64]{1,2,0:T(8,128)(2,1)} %param.31) | copy-start | bytes 786436
  57.5 26.1 %all-to-all-start = ((bf16[2,64,96]{2,0,1:T(2,128)(2,1)}), bf16[2,64,96]{2,0,1:T(2,128)(2,1)S(1)}, u32[]{:S(2)}, u32[]{:S(2)}) async-start(bf16[2,64,96]{2,0,1:T(2,128)(2,1)} %copy.88), calls=%async_computation | async-start | bytes 65536 | tf_op jit(solution)/shard_map/all_to_all | solution.py:83
  83.6 21.2 %all-to-all-start.8 = ((bf16[64,2,512]{2,1,0:T(2,128)(2,1)}), bf16[64,2,512]{2,1,0:T(2,128)(2,1)S(1)}, u32[]{:S(2)}, u32[]{:S(2)}) async-start(bf16[64,2,512]{2,1,0:T(2,128)(2,1)} %reshape.580), calls=%async_computation.8 | async-start | bytes 262144 | tf_op jit(solution)/shard_map/all_to_all | solution.py:75
  104.8 18.8 %all-to-all-start.3 = ((bf16[64,1,12]{2,1,0:T(2,128)(2,1)}), bf16[64,1,12]{2,1,0:T(2,128)(2,1)S(1)}, u32[]{:S(2)}, u32[]{:S(2)}) async-start(bf16[64,1,12]{2,1,0:T(2,128)(2,1)} %copy.94), calls=%async_computation.3 | async-start | bytes 65536 | tf_op jit(solution)/shard_map/all_to_all | solution.py:96
  123.6 19.2 %all-to-all-start.1 = ((bf16[64,1,96]{2,1,0:T(2,128)(2,1)}), bf16[64,1,96]{2,1,0:T(2,128)(2,1)S(1)}, u32[]{:S(2)}, u32[]{:S(2)}) async-start(bf16[64,1,96]{2,1,0:T(2,128)(2,1)} %copy.89), calls=%async_computation.1 | async-start | bytes 65536 | tf_op jit(solution)/shard_map/all_to_all | solution.py:95
  130.8 40.3 %copy-start.1 = (bf16[2,32,64,128]{3,2,1,0:T(8,128)(2,1)S(1)}, bf16[2,32,64,128]{3,2,1,0:T(8,128)(2,1)}, u32[]{:S(2)}) copy-start(bf16[2,32,64,128]{3,2,1,0:T(8,128)(2,1)} %param.33) | copy-start | bytes 3145732
  142.9 20.9 %all-to-all-start.9 = ((bf16[64,2,512]{2,1,0:T(2,128)(2,1)}), bf16[64,2,512]{2,1,0:T(2,128)(2,1)S(1)}, u32[]{:S(2)}, u32[]{:S(2)}) async-start(bf16[64,2,512]{2,1,0:T(2,128)(2,1)} %reshape.582), calls=%async_computation.9 | async-start | bytes 262144 | tf_op jit(solution)/shard_map/all_to_all | solution.py:93
  164.4 24.0 %all-to-all-start.6 = ((bf16[64,2,1024]{2,1,0:T(2,128)(2,1)}), bf16[64,2,1024]{2,1,0:T(2,128)(2,1)S(1)}, u32[]{:S(2)}, u32[]{:S(2)}) async-start(bf16[64,2,1024]{2,1,0:T(2,128)(2,1)} %reshape.584), calls=%async_computation.6 | async-start | bytes 524288 | tf_op jit(solution)/shard_map/all_to_all | solution.py:68
  171.6 23.0 %copy-start.20 = (f32[32]{0:T(128)S(1)}, f32[32]{0:T(128)}, u32[]{:S(2)}) copy-start(f32[32]{0:T(128)} %param.24) | copy-start | bytes 388
  171.6 23.0 %copy-start.16 = (bf16[256,32]{0,1:T(8,128)(2,1)S(1)}, bf16[256,32]{0,1:T(8,128)(2,1)}, u32[]{:S(2)}) copy-start(bf16[256,32]{0,1:T(8,128)(2,1)} %param.20) | copy-start | bytes 49156
  171.6 23.0 %copy-start.18 = (f32[32]{0:T(128)S(1)}, f32[32]{0:T(128)}, u32[]{:S(2)}) copy-start(f32[32]{0:T(128)} %param.23) | copy-start | bytes 388
  188.4 48.7 %all-to-all-start.4 = ((bf16[2,64,4096]{2,0,1:T(2,128)(2,1)}), bf16[2,64,4096]{2,0,1:T(2,128)(2,1)S(1)}, u32[]{:S(2)}, u32[]{:S(2)}) async-start(bf16[2,64,4096]{2,0,1:T(2,128)(2,1)} %copy.100), calls=%async_computation.4 | async-start | bytes 2097152 | tf_op jit(solution)/shard_map/all_to_all | solution.py:82
  237.1 23.3 %all-to-all-start.7 = ((bf16[64,2,1024]{2,1,0:T(2,128)(2,1)}), bf16[64,2,1024]{2,1,0:T(2,128)(2,1)S(1)}, u32[]{:S(2)}, u32[]{:S(2)}) async-start(bf16[64,2,1024]{2,1,0:T(2,128)(2,1)} %reshape.586), calls=%async_computation.7 | async-start | bytes 524288 | tf_op jit(solution)/shard_map/all_to_all | solution.py:92
  244.6 21.8 %copy-start.10 = (f32[2048]{0:T(1024)S(1)}, f32[2048]{0:T(1024)}, u32[]{:S(2)}) copy-start(f32[2048]{0:T(1024)} %param.26) | copy-start | bytes 24580
  244.7 24.4 %copy-start.8 = (bf16[256,1,2,128]{3,2,1,0:T(2,128)(2,1)S(1)}, bf16[256,1,2,128]{3,2,1,0:T(2,128)(2,1)}, u32[]{:S(2)}) copy-start(bf16[256,1,2,128]{3,2,1,0:T(2,128)(2,1)} %param.19) | copy-start | bytes 393220
  244.7 24.4 %copy-start.2 = (bf16[256,2048]{1,0:T(8,128)(2,1)S(1)}, bf16[256,2048]{1,0:T(8,128)(2,1)}, u32[]{:S(2)}) copy-start(bf16[256,2048]{1,0:T(8,128)(2,1)} %param.18) | copy-start | bytes 3145732
  247.0 23.3 %copy-start.17 = (f32[4,1,2,128]{3,2,1,0:T(2,128)S(1)}, f32[4,1,2,128]{3,2,1,0:T(2,128)}, u32[]{:S(2)}) copy-start(f32[4,1,2,128]{3,2,1,0:T(2,128)} %param.22) | copy-start | bytes 12292
  247.0 23.3 %copy-start.13 = (f32[4,2048]{1,0:T(4,128)S(1)}, f32[4,2048]{1,0:T(4,128)}, u32[]{:S(2)}) copy-start(f32[4,2048]{1,0:T(4,128)} %param.21) | copy-start | bytes 98308
  260.4 29.4 %all-to-all-start.5 = ((bf16[64,2,2048]{2,1,0:T(2,128)(2,1)}), bf16[64,2,2048]{2,1,0:T(2,128)(2,1)S(1)}, u32[]{:S(2)}, u32[]{:S(2)}) async-start(bf16[64,2,2048]{2,1,0:T(2,128)(2,1)} %reshape.578), calls=%async_computation.5 | async-start | bytes 1048576 | tf_op jit(solution)/shard_map/all_to_all | solution.py:94
  272.2 3.8 %copy-start.5 = (bf16[64,2,512]{2,1,0:T(2,128)(2,1)S(1)}, bf16[64,2,512]{2,1,0:T(2,128)(2,1)}, u32[]{:S(2)}) copy-start(bf16[64,2,512]{2,1,0:T(2,128)(2,1)} %copy-done.4) | copy-start | bytes 393220
  323.3 1.9 copy-start.11
  325.2 2.8 copy-start
  325.2 2.8 copy-start.19
  (8 other events, 9.3 us)
where the time goes:
time: 331 us; the launch traced here: 330 us
  waiting for transfers between devices  137 us (41%)
  starting transfers between devices  81.3 us (25%)
  blocking collectives  49.5 us (15%)
  local copies, waits for them, and re-layouts  30.2 us (9%)
  other arithmetic  21.9 us (7%)
  matrix products  7.25 us (2%)
    all_to_all x1, waiting for transfers between devices, per_device(): lax.all_to_all(ssm_flat, 'req', split_axis=1, concat_axis=0, tiled=True)  38.3 us
    unnamed x1, blocking collectives  25 us
    psum x1, blocking collectives, per_device(): reduced_rank = lax.psum(low_partial, 'head').astype(jnp.bfloat16)  24.5 us
    all_to_all x1, starting transfers between devices, per_device(): lax.all_to_all(convbc_flat, 'req', split_axis=1, concat_axis=0, tiled=True)  18.6 us
    all_to_all x1, waiting for transfers between devices, per_device(): lax.all_to_all(adapter_down_panels.reshape(adapter_down_panels.shape[0],...  14.8 us
    unnamed x71, local copies, waits for them, and re-layouts  14.5 us
    all_to_all x1, waiting for transfers between devices, per_device(): lax.all_to_all(picked_left_factor, 'req', split_axis=0, concat_axis=1, ti...  13.4 us
    all_to_all x1, starting transfers between devices, per_device(): lax.all_to_all(convx_flat, 'req', split_axis=1, concat_axis=0, tiled=True)  13.3 us
  transfers between devices with their start and end apart: 10, of which 9 were waited for; matrix products, arithmetic and copies ran while one was open for 12% of the time, Pallas kernels for 0%

commit v1 on v0

--- a/solution.py
+++ b/solution.py
@@ -5,6 +5,15 @@
 
 ADAPTER_SCALE = 2.0
 NORM_EPSILON = 1e-05
+
+
+def store_the_windows(patch, row_dim, dim_i):
+    return jnp.concatenate(
+        lax.all_to_all(
+            jnp.stack(jnp.split(patch, lax.axis_size("req"), axis=row_dim)), "req", 0, 0
+        ),
+        axis=dim_i,
+    )
 
 
 def causal_conv(cached, current, weight):
@@ -92,7 +101,7 @@
         lax.all_to_all(picked_left_factor, "req", split_axis=0, concat_axis=1, tiled=True),
         lax.all_to_all(picked_right_factor, "req", split_axis=0, concat_axis=1, tiled=True),
         lax.all_to_all(chosen_state, "req", split_axis=0, concat_axis=1, tiled=True),
-        lax.all_to_all(chosen_convx, "req", split_axis=0, concat_axis=1, tiled=True),
+        store_the_windows(chosen_convx, 0, 1),
         lax.all_to_all(chosen_convbc, "req", split_axis=0, concat_axis=1, tiled=True),
     )
     down_panel = fetched[0].reshape(per_device_share, hidden_features_on_card, reduced_width)

time: 331 us -> 360 us (1.088)
  the two profiles are of different devices: /device:TPU:16 before, /device:TPU:8 now
where the time goes in v1:
time: 360 us; the launch traced here: 359 us
  waiting for transfers between devices  128 us (36%)
  starting transfers between devices  84.8 us (24%)
  local copies, waits for them, and re-layouts  62.4 us (17%)
  blocking collectives  51 us (14%)
  other arithmetic  21.9 us (6%)
  matrix products  7.24 us (2%)
    unnamed x134, local copies, waits for them, and re-layouts  46.9 us
    all_to_all x1, waiting for transfers between devices, per_device(): lax.all_to_all(ssm_flat, 'req', split_axis=1, concat_axis=0, tiled=True)  38.8 us
    unnamed x1, blocking collectives  26.5 us
    psum x1, blocking collectives, per_device(): reduced_rank = lax.psum(low_partial, 'head').astype(jnp.bfloat16)  24.5 us
    all_to_all x1, starting transfers between devices, per_device(): lax.all_to_all(convbc_flat, 'req', split_axis=1, concat_axis=0, tiled=True)  18.7 us
    all_to_all x1, waiting for transfers between devices, per_device(): lax.all_to_all(adapter_down_panels.reshape(adapter_down_panels.shape[0],...  15.3 us
    all_to_all x1, starting transfers between devices, per_device(): lax.all_to_all(chosen_convbc, 'req', split_axis=0, concat_axis=1, tiled=T...  15.2 us
    all_to_all x1, waiting for transfers between devices, per_device(): lax.all_to_all(picked_left_factor, 'req', split_axis=0, concat_axis=1, ti...  13.9 us
  transfers between devices with their start and end apart: 10, of which 8 were waited for; matrix products, arithmetic and copies ran while one was open for 20% of the time, Pallas kernels for 0%

profile of v1, /device:TPU:8, one launch (start us, length us, event | category | flops | bytes accessed | tf_op | source)
XLA Modules:
  0.0 358.5 jit_solution(16805403306066026485)
XLA Ops:
  2.1 18.7 %all-to-all-start.2 = ((bf16[2,64,12]{2,0,1:T(2,128)(2,1)}), bf16[2,64,12]{2,0,1:T(2,128)(2,1)S(1)}, u32[]{:S(2)}, u32[]{:S(2)}) async-start(bf16[2,64,12]{2,0,1:T(2,128)(2,1)} %copy.91), calls=%async_computation.2 | async-start | bytes 65536 | tf_op jit(solution)/shard_map/all_to_all | solution.py:93
  26.3 26.5 %all-reduce.3 = (s32[64]{0:T(128)S(1)}, s32[64]{0:T(128)S(1)}, s32[64]{0:T(128)S(1)}) all-reduce(s32[64]{0:T(128)S(1)} %dynamic-update-slice.1, s32[64]{0:T(128)S(1)} %dynamic-update-slice, s32[64]{0:T(128)S(1)} %dynamic-update-slice.2), channel_id=1, replica_groups=mesh['req'=64,'head'=8] {'req'}, use_global_device_ids=true, to_apply=%add.1 | all-reduce | flops 192 | bytes 1536
  59.1 11.8 %all-to-all-start = ((bf16[2,64,96]{2,0,1:T(2,128)(2,1)}), bf16[2,64,96]{2,0,1:T(2,128)(2,1)S(1)}, u32[]{:S(2)}, u32[]{:S(2)}) async-start(bf16[2,64,96]{2,0,1:T(2,128)(2,1)} %copy.87), calls=%async_computation | async-start | bytes 65536 | tf_op jit(solution)/shard_map/all_to_all | solution.py:92
  72.3 12.2 %all-to-all-done = bf16[2,64,96]{2,0,1:T(2,128)(2,1)S(1)} async-done(((bf16[2,64,96]{2,0,1:T(2,128)(2,1)}), bf16[2,64,96]{2,0,1:T(2,128)(2,1)S(1)}, u32[]{:S(2)}, u32[]{:S(2)}) %all-to-all-start) | async-done | bytes 24608 | tf_op jit(solution)/shard_map/all_to_all | solution.py:92
  84.5 5.5 %all-to-all-start.8 = ((bf16[64,2,512]{2,1,0:T(2,128)(2,1)}), bf16[64,2,512]{2,1,0:T(2,128)(2,1)S(1)}, u32[]{:S(2)}, u32[]{:S(2)}) async-start(bf16[64,2,512]{2,1,0:T(2,128)(2,1)} %reshape.545), calls=%async_computation.8 | async-start | bytes 262144 | tf_op jit(solution)/shard_map/all_to_all | solution.py:84
  123.1 15.2 %all-to-all-start.3 = ((bf16[64,1,12]{2,1,0:T(2,128)(2,1)}), bf16[64,1,12]{2,1,0:T(2,128)(2,1)S(1)}, u32[]{:S(2)}, u32[]{:S(2)}) async-start(bf16[64,1,12]{2,1,0:T(2,128)(2,1)} %copy.92), calls=%async_computation.3 | async-start | bytes 65536 | tf_op jit(solution)/shard_map/all_to_all | solution.py:105
  139.7 12.3 %all-to-all-done.3 = bf16[64,1,12]{2,1,0:T(2,128)(2,1)S(1)} async-done(((bf16[64,1,12]{2,1,0:T(2,128)(2,1)}), bf16[64,1,12]{2,1,0:T(2,128)(2,1)S(1)}, u32[]{:S(2)}, u32[]{:S(2)}) %all-to-all-start.3) | async-done | bytes 1568 | tf_op jit(solution)/shard_map/all_to_all | solution.py:105
  152.1 5.3 %all-to-all-start.1 = ((bf16[64,1,96]{2,1,0:T(2,128)(2,1)}), bf16[64,1,96]{2,1,0:T(2,128)(2,1)S(1)}, u32[]{:S(2)}, u32[]{:S(2)}) async-start(bf16[64,1,96]{2,1,0:T(2,128)(2,1)} %constant_dynamic-update-slice_fusion), calls=%async_computation.1 | async-start | bytes 65536 | tf_op jit(solution)/shard_map/all_to_all | solution.py:12
  158.9 12.1 %all-to-all-done.1 = bf16[64,1,96]{2,1,0:T(2,128)(2,1)S(1)} async-done(((bf16[64,1,96]{2,1,0:T(2,128)(2,1)}), bf16[64,1,96]{2,1,0:T(2,128)(2,1)S(1)}, u32[]{:S(2)}, u32[]{:S(2)}) %all-to-all-start.1) | async-done | bytes 12320 | tf_op jit(solution)/shard_map/all_to_all | solution.py:12
  171.0 5.6 %all-to-all-start.9 = ((bf16[64,2,512]{2,1,0:T(2,128)(2,1)}), bf16[64,2,512]{2,1,0:T(2,128)(2,1)S(1)}, u32[]{:S(2)}, u32[]{:S(2)}) async-start(bf16[64,2,512]{2,1,0:T(2,128)(2,1)} %reshape.547), calls=%async_computation.9 | async-start | bytes 262144 | tf_op jit(solution)/shard_map/all_to_all | solution.py:102
  180.4 11.7 %all-to-all-done.9 = bf16[64,2,512]{2,1,0:T(2,128)(2,1)S(1)} async-done(((bf16[64,2,512]{2,1,0:T(2,128)(2,1)}), bf16[64,2,512]{2,1,0:T(2,128)(2,1)S(1)}, u32[]{:S(2)}, u32[]{:S(2)}) %all-to-all-start.9) | async-done | bytes 131104 | tf_op jit(solution)/shard_map/all_to_all | solution.py:102
  192.7 5.8 %all-to-all-start.6 = ((bf16[64,2,1024]{2,1,0:T(2,128)(2,1)}), bf16[64,2,1024]{2,1,0:T(2,128)(2,1)S(1)}, u32[]{:S(2)}, u32[]{:S(2)}) async-start(bf16[64,2,1024]{2,1,0:T(2,128)(2,1)} %reshape.549), calls=%async_computation.6 | async-start | bytes 524288 | tf_op jit(solution)/shard_map/all_to_all | solution.py:77
  201.1 15.3 %all-to-all-done.6 = bf16[64,2,1024]{2,1,0:T(2,128)(2,1)S(1)} async-done(((bf16[64,2,1024]{2,1,0:T(2,128)(2,1)}), bf16[64,2,1024]{2,1,0:T(2,128)(2,1)S(1)}, u32[]{:S(2)}, u32[]{:S(2)}) %all-to-all-start.6) | async-done | bytes 262176 | tf_op jit(solution)/shard_map/all_to_all | solution.py:77
  216.3 5.6 %all-to-all-start.4 = ((bf16[2,64,4096]{2,0,1:T(2,128)(2,1)}), bf16[2,64,4096]{2,0,1:T(2,128)(2,1)S(1)}, u32[]{:S(2)}, u32[]{:S(2)}) async-start(bf16[2,64,4096]{2,0,1:T(2,128)(2,1)} %copy.98), calls=%async_computation.4 | async-start | bytes 2097152 | tf_op jit(solution)/shard_map/all_to_all | solution.py:91
  226.2 38.8 %all-to-all-done.4 = bf16[2,64,4096]{2,0,1:T(2,128)(2,1)S(1)} async-done(((bf16[2,64,4096]{2,0,1:T(2,128)(2,1)}), bf16[2,64,4096]{2,0,1:T(2,128)(2,1)S(1)}, u32[]{:S(2)}, u32[]{:S(2)}) %all-to-all-start.4) | async-done | bytes 1048608 | tf_op jit(solution)/shard_map/all_to_all | solution.py:91
  265.0 5.9 %all-to-all-start.7 = ((bf16[64,2,1024]{2,1,0:T(2,128)(2,1)}), bf16[64,2,1024]{2,1,0:T(2,128)(2,1)S(1)}, u32[]{:S(2)}, u32[]{:S(2)}) async-start(bf16[64,2,1024]{2,1,0:T(2,128)(2,1)} %reshape.551), calls=%async_computation.7 | async-start | bytes 524288 | tf_op jit(solution)/shard_map/all_to_all | solution.py:101
  274.9 13.9 %all-to-all-done.7 = bf16[64,2,1024]{2,1,0:T(2,128)(2,1)S(1)} async-done(((bf16[64,2,1024]{2,1,0:T(2,128)(2,1)}), bf16[64,2,1024]{2,1,0:T(2,128)(2,1)S(1)}, u32[]{:S(2)}, u32[]{:S(2)}) %all-to-all-start.7) | async-done | bytes 262176 | tf_op jit(solution)/shard_map/all_to_all | solution.py:101
  288.8 5.4 %all-to-all-start.5 = ((bf16[64,2,2048]{2,1,0:T(2,128)(2,1)}), bf16[64,2,2048]{2,1,0:T(2,128)(2,1)S(1)}, u32[]{:S(2)}, u32[]{:S(2)}) async-start(bf16[64,2,2048]{2,1,0:T(2,128)(2,1)} %reshape.543), calls=%async_computation.5 | async-start | bytes 1048576 | tf_op jit(solution)/shard_map/all_to_all | solution.py:103
  300.1 3.8 %fusion.9 = (bf16[1,256,2048]{1,2,0:T(8,128)(2,1)}, bf16[1,256,2048]{1,2,0:T(8,128)(2,1)}) fusion(f32[256,32]{0,1:T(8,128)S(1)} %bitcast.419, bf16[256,2048]{0,1:T(8,128)(2,1)S(1)} %copy.88, f32[2048]{0:T(1024)S(1)} %bitcast.423, bf16[1,256,2048]{1,2,0:T(8,128)(2,1)S(1)} %bitcast.401, bf16[1,3,2048]{1,2,0:T(8,128)(2,1)S(1)} %copy.89, f32[2048]{0:T(1024)S(1)} %bitcast.424, ...), kind=kLoop, calls=%fused_computation.17 | loop fusion | flops 14680064 | bytes 4272128 | tf_op jit(solution)/shard_map/convert_element_type | solution.py:171
  306.3 11.7 %all-to-all-done.5 = bf16[64,2,2048]{2,1,0:T(2,128)(2,1)S(1)} async-done(((bf16[64,2,2048]{2,1,0:T(2,128)(2,1)}), bf16[64,2,2048]{2,1,0:T(2,128)(2,1)S(1)}, u32[]{:S(2)}, u32[]{:S(2)}) %all-to-all-start.5) | async-done | bytes 524320 | tf_op jit(solution)/shard_map/all_to_all | solution.py:103
  318.5 3.1 reduce.4
  323.0 2.6 multiply_reduce_fusion
  327.0 24.5 %psum.7 = bf16[1,256,64]{1,2,0:T(8,128)(2,1)S(1)} all-reduce(f32[1,256,64]{1,2,0:T(8,128)} %convolution_bitcast_fusion), channel_id=1, replica_groups=mesh['req'=64,'head'=8] {'head'}, use_global_device_ids=true, to_apply=%region_4.5 | all-reduce | flops 16384 | bytes 98304 | tf_op jit(solution)/shard_map/psum | solution.py:162
  353.3 2.8 multiply_convert_fusion.3
  (205 shorter events, 79.1 us)
Async XLA Ops:
  2.1 57.1 %all-to-all-start.2 = ((bf16[2,64,12]{2,0,1:T(2,128)(2,1)}), bf16[2,64,12]{2,0,1:T(2,128)(2,1)S(1)}, u32[]{:S(2)}, u32[]{:S(2)}) async-start(bf16[2,64,12]{2,0,1:T(2,128)(2,1)} %copy.91), calls=%async_computation.2 | async-start | bytes 65536 | tf_op jit(solution)/shard_map/all_to_all | solution.py:93
  58.4 118.2 %copy-start.6 = (bf16[1,2048,64]{1,2,0:T(8,128)(2,1)S(1)}, bf16[1,2048,64]{1,2,0:T(8,128)(2,1)}, u32[]{:S(2)}) copy-start(bf16[1,2048,64]{1,2,0:T(8,128)(2,1)} %param.31) | copy-start | bytes 786436
  59.1 25.3 %all-to-all-start = ((bf16[2,64,96]{2,0,1:T(2,128)(2,1)}), bf16[2,64,96]{2,0,1:T(2,128)(2,1)S(1)}, u32[]{:S(2)}, u32[]{:S(2)}) async-start(bf16[2,64,96]{2,0,1:T(2,128)(2,1)} %copy.87), calls=%async_computation | async-start | bytes 65536 | tf_op jit(solution)/shard_map/all_to_all | solution.py:92
  84.5 38.7 %all-to-all-start.8 = ((bf16[64,2,512]{2,1,0:T(2,128)(2,1)}), bf16[64,2,512]{2,1,0:T(2,128)(2,1)S(1)}, u32[]{:S(2)}, u32[]{:S(2)}) async-start(bf16[64,2,512]{2,1,0:T(2,128)(2,1)} %reshape.545), calls=%async_computation.8 | async-start | bytes 262144 | tf_op jit(solution)/shard_map/all_to_all | solution.py:84
  123.1 28.9 %all-to-all-start.3 = ((bf16[64,1,12]{2,1,0:T(2,128)(2,1)}), bf16[64,1,12]{2,1,0:T(2,128)(2,1)S(1)}, u32[]{:S(2)}, u32[]{:S(2)}) async-start(bf16[64,1,12]{2,1,0:T(2,128)(2,1)} %copy.92), calls=%async_computation.3 | async-start | bytes 65536 | tf_op jit(solution)/shard_map/all_to_all | solution.py:105
  152.1 18.9 %all-to-all-start.1 = ((bf16[64,1,96]{2,1,0:T(2,128)(2,1)}), bf16[64,1,96]{2,1,0:T(2,128)(2,1)S(1)}, u32[]{:S(2)}, u32[]{:S(2)}) async-start(bf16[64,1,96]{2,1,0:T(2,128)(2,1)} %constant_dynamic-update-slice_fusion), calls=%async_computation.1 | async-start | bytes 65536 | tf_op jit(solution)/shard_map/all_to_all | solution.py:12
  158.2 40.3 %copy-start.1 = (bf16[2,32,64,128]{3,2,1,0:T(8,128)(2,1)S(1)}, bf16[2,32,64,128]{3,2,1,0:T(8,128)(2,1)}, u32[]{:S(2)}) copy-start(bf16[2,32,64,128]{3,2,1,0:T(8,128)(2,1)} %param.33) | copy-start | bytes 3145732
  171.0 21.0 %all-to-all-start.9 = ((bf16[64,2,512]{2,1,0:T(2,128)(2,1)}), bf16[64,2,512]{2,1,0:T(2,128)(2,1)S(1)}, u32[]{:S(2)}, u32[]{:S(2)}) async-start(bf16[64,2,512]{2,1,0:T(2,128)(2,1)} %reshape.547), calls=%async_computation.9 | async-start | bytes 262144 | tf_op jit(solution)/shard_map/all_to_all | solution.py:102
  192.7 23.7 %all-to-all-start.6 = ((bf16[64,2,1024]{2,1,0:T(2,128)(2,1)}), bf16[64,2,1024]{2,1,0:T(2,128)(2,1)S(1)}, u32[]{:S(2)}, u32[]{:S(2)}) async-start(bf16[64,2,1024]{2,1,0:T(2,128)(2,1)} %reshape.549), calls=%async_computation.6 | async-start | bytes 524288 | tf_op jit(solution)/shard_map/all_to_all | solution.py:77
  199.0 23.0 %copy-start.20 = (f32[32]{0:T(128)S(1)}, f32[32]{0:T(128)}, u32[]{:S(2)}) copy-start(f32[32]{0:T(128)} %param.24) | copy-start | bytes 388
  199.0 23.0 %copy-start.16 = (bf16[256,32]{0,1:T(8,128)(2,1)S(1)}, bf16[256,32]{0,1:T(8,128)(2,1)}, u32[]{:S(2)}) copy-start(bf16[256,32]{0,1:T(8,128)(2,1)} %param.20) | copy-start | bytes 49156
  199.0 23.0 %copy-start.18 = (f32[32]{0:T(128)S(1)}, f32[32]{0:T(128)}, u32[]{:S(2)}) copy-start(f32[32]{0:T(128)} %param.23) | copy-start | bytes 388
  216.3 48.7 %all-to-all-start.4 = ((bf16[2,64,4096]{2,0,1:T(2,128)(2,1)}), bf16[2,64,4096]{2,0,1:T(2,128)(2,1)S(1)}, u32[]{:S(2)}, u32[]{:S(2)}) async-start(bf16[2,64,4096]{2,0,1:T(2,128)(2,1)} %copy.98), calls=%async_computation.4 | async-start | bytes 2097152 | tf_op jit(solution)/shard_map/all_to_all | solution.py:91
  265.0 23.8 %all-to-all-start.7 = ((bf16[64,2,1024]{2,1,0:T(2,128)(2,1)}), bf16[64,2,1024]{2,1,0:T(2,128)(2,1)S(1)}, u32[]{:S(2)}, u32[]{:S(2)}) async-start(bf16[64,2,1024]{2,1,0:T(2,128)(2,1)} %reshape.551), calls=%async_computation.7 | async-start | bytes 524288 | tf_op jit(solution)/shard_map/all_to_all | solution.py:101
  272.4 21.8 %copy-start.10 = (f32[2048]{0:T(1024)S(1)}, f32[2048]{0:T(1024)}, u32[]{:S(2)}) copy-start(f32[2048]{0:T(1024)} %param.26) | copy-start | bytes 24580
  272.6 24.4 %copy-start.8 = (bf16[256,1,2,128]{3,2,1,0:T(2,128)(2,1)S(1)}, bf16[256,1,2,128]{3,2,1,0:T(2,128)(2,1)}, u32[]{:S(2)}) copy-start(bf16[256,1,2,128]{3,2,1,0:T(2,128)(2,1)} %param.19) | copy-start | bytes 393220
  272.6 24.4 %copy-start.2 = (bf16[256,2048]{1,0:T(8,128)(2,1)S(1)}, bf16[256,2048]{1,0:T(8,128)(2,1)}, u32[]{:S(2)}) copy-start(bf16[256,2048]{1,0:T(8,128)(2,1)} %param.18) | copy-start | bytes 3145732
  274.9 23.3 %copy-start.17 = (f32[4,1,2,128]{3,2,1,0:T(2,128)S(1)}, f32[4,1,2,128]{3,2,1,0:T(2,128)}, u32[]{:S(2)}) copy-start(f32[4,1,2,128]{3,2,1,0:T(2,128)} %param.22) | copy-start | bytes 12292
  274.9 23.3 %copy-start.13 = (f32[4,2048]{1,0:T(4,128)S(1)}, f32[4,2048]{1,0:T(4,128)}, u32[]{:S(2)}) copy-start(f32[4,2048]{1,0:T(4,128)} %param.21) | copy-start | bytes 98308
  288.8 29.2 %all-to-all-start.5 = ((bf16[64,2,2048]{2,1,0:T(2,128)(2,1)}), bf16[64,2,2048]{2,1,0:T(2,128)(2,1)S(1)}, u32[]{:S(2)}, u32[]{:S(2)}) async-start(bf16[64,2,2048]{2,1,0:T(2,128)(2,1)} %reshape.543), calls=%async_computation.5 | async-start | bytes 1048576 | tf_op jit(solution)/shard_map/all_to_all | solution.py:103
  300.1 3.8 %copy-start.5 = (bf16[64,2,512]{2,1,0:T(2,128)(2,1)S(1)}, bf16[64,2,512]{2,1,0:T(2,128)(2,1)}, u32[]{:S(2)}) copy-start(bf16[64,2,512]{2,1,0:T(2,128)(2,1)} %copy-done.4) | copy-start | bytes 393220
  351.5 1.9 copy-start.11
  353.3 2.8 copy-start
  353.3 2.8 copy-start.19
  (8 other events, 9.3 us)
